TPU v7x, 128 devices: a whole 4x4x4 slice. The times are simulated.
128 devices in a mesh: inp: 2 (over z_hi), tm: 64 (over z_lo, x, y, core).
Axes of the slice: x: 4, y: 4, z: 4 (z_hi: 2, z_lo: 2; z = z_hi * 2 + z_lo), core: 2. Of those that a mesh axis runs over, the one named last changes fastest.
Arguments:
- raw: bfloat16 [1024, 524288], P('inp', 'tm'), may hold values from -6 to 6
- taps: float32 [4, 512], replicated, may hold values from -3 to 3
Outputs:
- visibilities: float32 [256, 2, 1024, 1024], P('tm', None, 'inp')
All inputs are finite; a program needn't handle non-finite values.
Results may differ from a plain program's by a relative error of at most 0.0052.
Values may be sent and summed in bfloat16 or wider, within the bound.
A program may use at most 192 MiB of HBM per device.

v0:
```python
import math

import jax
import jax.numpy as jnp
from jax import lax
from jax.sharding import PartitionSpec as P


def from_behind(value, axis, by):
    devices = lax.axis_size(axis)
    pairs = [(i, i + by) for i in range(devices) if 0 <= i + by < devices]
    return lax.ppermute(value, axis, pairs)


def from_partner(value, axis, stride):
    return lax.ppermute(value, axis, [(i, i ^ 1 << stride) for i in range(lax.axis_size(axis))])


def dft_table(length):
    half = length // 2
    kidx = jnp.arange(half, dtype=jnp.int32)[:, None]
    nidx = jnp.arange(length, dtype=jnp.int32)[None, :]
    phase = (kidx * nidx % length).astype(jnp.float32) * (2.0 * math.pi / length)
    norm = 1.0 / math.sqrt(length)
    return jnp.stack([jnp.cos(phase) * norm, -jnp.sin(phase) * norm], axis=1).astype(jnp.bfloat16)


def cross_power(rows, cols, count):
    rotated = jnp.stack([cols[:, 1], -cols[:, 0]], axis=1)
    real_part = jnp.einsum("crsi,crsj->cij", rows, cols, preferred_element_type=jnp.float32)
    imag_part = jnp.einsum("crsi,crsj->cij", rows, rotated, preferred_element_type=jnp.float32)
    return jnp.stack([real_part, imag_part], axis=1) / count


def per_device(raw, taps):
    n_taps, length = taps.shape
    block_inputs, local_samples = raw.shape
    spec_local = local_samples // length
    frames = raw.reshape(block_inputs, spec_local, length)
    tail = frames[:, spec_local - (n_taps - 1) :, :]
    before = from_behind(tail, "tm", 1)
    extended = jnp.concatenate([before, frames], axis=1)
    filtered = sum(
        (taps[t][None, None, :] * extended[:, t : t + spec_local, :] for t in range(n_taps))
    )
    filtered = filtered.astype(jnp.bfloat16)
    table = dft_table(length)
    spectra = jnp.einsum(
        "isn,crn->crsi", filtered, table, preferred_element_type=jnp.float32
    ).astype(jnp.bfloat16)
    turned = lax.all_to_all(spectra, "tm", split_axis=0, concat_axis=2, tiled=True)
    count = turned.shape[2]
    group = lax.axis_index("inp")
    first = group == 0
    other = from_partner(turned, "inp", 0)
    leading = jnp.where(first, turned, other)
    trailing = jnp.where(first, other, turned)
    columns = jnp.concatenate([leading, trailing], axis=3)
    return cross_power(turned, columns, count)


def solution(mesh):
    return jax.shard_map(
        per_device,
        mesh=mesh,
        in_specs=(P("inp", "tm"), P()),
        out_specs=P("tm", None, "inp", None),
        check_vma=False,
    )
```

profile of v0, /device:TPU:1, one launch (start us, length us, event | category | flops | bytes accessed | tf_op | source)
XLA Modules:
  0.0 431.0 jit_solution(877422707255545557)
XLA Ops:
  0.0 0.0 copy-start.2
  0.0 7.7 %copy.30 = bf16[64,16,8,512]{3,2,0,1:T(8,128)(2,1)} copy(bf16[64,16,8,512]{3,2,1,0:T(8,128)(2,1)} %bitcast.44) | data formatting | bytes 16777216 | tf_op jit(solution)/shard_map/reshape | solution.py:39
  7.7 1.5 slice.40
  9.2 4.6 %collective-permute-start = (bf16[512,3,512]{2,0,1:T(8,128)(2,1)S(1)}, bf16[512,3,512]{2,0,1:T(8,128)(2,1)S(1)}, u32[]{:S(2)}, u32[]{:S(2)}) collective-permute-start(bf16[512,3,512]{2,0,1:T(8,128)(2,1)S(1)} %slice.40), channel_id=1, source_target_pairs={{0,1},{1,2},{2,3},{3,4},{4,5},{5,6},{6,7},{7,8},{8,9},{9,10},{10,1... | collective-permute-start | bytes 4718600 | tf_op jit(solution)/shard_map/ppermute | solution.py:12
  13.8 2.2 multiply_convert_fusion
  16.0 0.0 copy-done.2
  16.0 15.1 %collective-permute-done = bf16[512,3,512]{2,0,1:T(8,128)(2,1)S(1)} collective-permute-done((bf16[512,3,512]{2,0,1:T(8,128)(2,1)S(1)}, bf16[512,3,512]{2,0,1:T(8,128)(2,1)S(1)}, u32[]{:S(2)}, u32[]{:S(2)}) %collective-permute-start) | collective-permute-done | bytes 1572896 | tf_op jit(solution)/shard_map/ppermute | solution.py:12
  31.1 1.2 constant_dynamic-update-slice_fusion.1
  32.4 7.7 %constant_dynamic-update-slice_fusion = bf16[512,19,512]{2,0,1:T(8,128)(2,1)} fusion(bf16[512,19,512]{2,0,1:T(8,128)(2,1)} %constant_dynamic-update-slice_fusion.1, bf16[64,16,8,512]{3,2,1,0:T(8,128)(2,1)} %bitcast.45), kind=kLoop, calls=%fused_computation.42 | loop fusion | bytes 16777216 | tf_op jit(solution)/shard_map/concatenate | solution.py:42
  40.1 16.6 %convert_bitcast_fusion = bf16[256,2,16,512]{3,0,2,1:T(8,128)(2,1)} fusion(bf16[512,19,512]{2,0,1:T(8,128)(2,1)} %constant_dynamic-update-slice_fusion, f32[512]{0:T(512)S(1)} %bitcast.51, f32[512]{0:T(512)S(1)} %bitcast.52, f32[512]{0:T(512)S(1)} %bitcast.50, f32[512]{0:T(512)S(1)} %bitcast.49, bf16[256,1,512]{2,0,1:T(8,128)(2,1)S(1)} %get-tuple-element.13, ...), kind=kOutput, calls=%fused_computation.19 | convolution fusion | flops 4350541824 | bytes 42475520 | tf_op jit(solution)/shard_map/isn,crn->crsi/dot_general | solution.py:48
  56.7 11.5 %copy.13 = bf16[256,2,16,512]{3,2,1,0:T(8,128)(2,1)} copy(bf16[256,2,16,512]{3,0,2,1:T(8,128)(2,1)} %convert_bitcast_fusion) | data formatting | bytes 16777216 | tf_op jit(solution)/shard_map/convert_element_type | solution.py:50
  68.2 107.7 %all_to_all.18 = bf16[256,2,16,512]{3,2,1,0:T(8,128)(2,1)} all-to-all(bf16[256,2,16,512]{3,2,1,0:T(8,128)(2,1)} %copy.13), channel_id=1, replica_groups=mesh['inp'=2,'tm'=64] {'tm'}, dimensions={0} | all-to-all | bytes 16777216 | tf_op jit(solution)/shard_map/all_to_all | solution.py:51
  175.9 8.1 %copy.14 = bf16[64,4,2,16,512]{4,3,0,2,1:T(8,128)(2,1)} copy(bf16[64,4,2,16,512]{4,3,2,1,0:T(8,128)(2,1)} %bitcast.47) | data formatting | bytes 16777216 | tf_op jit(solution)/shard_map/all_to_all | solution.py:51
  184.0 3.3 collective-permute-start.1
  187.3 180.1 %collective-permute-done.1 = bf16[4,2,1024,512]{3,2,1,0:T(8,128)(2,1)} collective-permute-done((bf16[4,2,1024,512]{3,2,1,0:T(8,128)(2,1)}, bf16[4,2,1024,512]{3,2,1,0:T(8,128)(2,1)}, u32[]{:S(2)}, u32[]{:S(2)}) %collective-permute-start.1) | collective-permute-done | bytes 8388640 | tf_op jit(solution)/shard_map/ppermute | solution.py:16
  367.4 6.5 %broadcast_select_fusion = (bf16[4,2,1024,512]{3,2,1,0:T(8,128)(2,1)S(1)}, bf16[4,2,1024,512]{3,2,1,0:T(8,128)(2,1)S(1)}) fusion(bf16[4,2,1024,512]{3,2,1,0:T(8,128)(2,1)} %collective-permute-done.1, pred[]{:T(512)S(6)} %eq.5, bf16[64,4,2,16,512]{4,3,0,2,1:T(8,128)(2,1)} %copy.14), kind=kLoop, calls=%fused_computation.24 | loop fusion | flops 8388608 | bytes 33554432 | tf_op jit(solution)/shard_map/jit(_where)/select_n | solution.py:57
  373.9 0.0 copy-start
  373.9 0.0 copy-start.1
  373.9 3.2 copy-done
  377.1 2.5 copy-done.1
  379.6 7.0 %fusion.6 = (bf16[4,1,1024,1024]{3,2,1,0:T(8,128)(2,1)}, bf16[4,1,1024,1024]{3,2,1,0:T(8,128)(2,1)}) fusion(bf16[4,2,1024,512]{3,2,1,0:T(8,128)(2,1)S(1)} %get-tuple-element.8, bf16[4,2,1024,512]{3,2,1,0:T(8,128)(2,1)S(1)} %get-tuple-element.7), kind=kLoop, calls=%fused_computation.13 | loop fusion | flops 37748736 | bytes 33554432 | tf_op jit(solution)/shard_map/concatenate | solution.py:58
  386.6 15.7 %fusion.21 = f32[4,1,512,1024]{3,2,0,1:T(8,128)} fusion(bf16[4,2,1024,512]{3,2,1,0:T(8,128)(2,1)} %bitcast.42, bf16[4,2,1024,512]{3,2,1,0:T(8,128)(2,1)} %copy-done, bf16[4,2,1024,512]{3,2,1,0:T(8,128)(2,1)} %copy-done.1), kind=kOutput, calls=%fused_computation.27 | convolution fusion | flops 8623489024 | bytes 33554432 | tf_op jit(solution)/shard_map/crsi,crsj->cij/dot_general | solution.py:30
  402.3 15.7 %fusion.18 = f32[4,1,512,1024]{3,2,0,1:T(8,128)} fusion(bf16[4,2,1024,512]{3,2,1,0:T(8,128)(2,1)} %bitcast.43, bf16[4,1,1024,1024]{3,2,1,0:T(8,128)(2,1)} %get-tuple-element.6, bf16[4,1,1024,1024]{3,2,1,0:T(8,128)(2,1)} %get-tuple-element.5), kind=kOutput, calls=%fused_computation.26 | convolution fusion | flops 8598323200 | bytes 33554432 | tf_op jit(solution)/shard_map/crsi,crsj->cij/dot_general | solution.py:31
  418.0 6.8 %maximum_multiply_fusion = f32[4,2,512,1024]{3,2,0,1:T(8,128)S(1)} fusion(f32[4,1,512,1024]{3,2,0,1:T(8,128)} %fusion.18, f32[4,1,512,1024]{3,2,0,1:T(8,128)} %fusion.21), kind=kLoop, calls=%fused_computation.10 | loop fusion | flops 8388608 | bytes 33554432 | tf_op jit(solution)/shard_map/div | solution.py:32
  424.8 6.2 %copy.17 = f32[4,2,512,1024]{3,2,1,0:T(8,128)} copy(f32[4,2,512,1024]{3,2,0,1:T(8,128)S(1)} %maximum_multiply_fusion) | data formatting | bytes 33554432 | tf_op jit(solution)/shard_map/div | solution.py:32
  (1 shorter events, 0.0 us)
Async XLA Ops:
  0.0 16.0 %copy-start.2 = (f32[4,512]{1,0:T(4,128)S(1)}, f32[4,512]{1,0:T(4,128)}, u32[]{:S(2)}) copy-start(f32[4,512]{1,0:T(4,128)} %param.3) | copy-start | bytes 24580
  9.2 21.9 %collective-permute-start = (bf16[512,3,512]{2,0,1:T(8,128)(2,1)S(1)}, bf16[512,3,512]{2,0,1:T(8,128)(2,1)S(1)}, u32[]{:S(2)}, u32[]{:S(2)}) collective-permute-start(bf16[512,3,512]{2,0,1:T(8,128)(2,1)S(1)} %slice.40), channel_id=1, source_target_pairs={{0,1},{1,2},{2,3},{3,4},{4,5},{5,6},{6,7},{7,8},{8,9},{9,10},{10,1... | collective-permute-start | bytes 4718600 | tf_op jit(solution)/shard_map/ppermute | solution.py:12
  184.0 183.4 %collective-permute-start.1 = (bf16[4,2,1024,512]{3,2,1,0:T(8,128)(2,1)}, bf16[4,2,1024,512]{3,2,1,0:T(8,128)(2,1)}, u32[]{:S(2)}, u32[]{:S(2)}) collective-permute-start(bf16[4,2,1024,512]{3,2,1,0:T(8,128)(2,1)} %bitcast.41), channel_id=1, source_target_pairs={{0,64},{64,0},{1,65},{65,1},{2,66},{66,2},{3,67},{67,3},{4,68},{68... | collective-permute-start | bytes 25165832 | tf_op jit(solution)/shard_map/ppermute | solution.py:16
  373.9 3.2 copy-start
  373.9 5.7 %copy-start.1 = (bf16[4,2,1024,512]{3,2,1,0:T(8,128)(2,1)}, bf16[4,2,1024,512]{3,2,1,0:T(8,128)(2,1)S(1)}, u32[]{:S(2)}) copy-start(bf16[4,2,1024,512]{3,2,1,0:T(8,128)(2,1)S(1)} %get-tuple-element.8) | copy-start | bytes 25165828
where the time goes:
time: 431 us
  waiting for transfers between devices  195 us (45%)
  blocking collectives  108 us (25%)
  local copies, waits for them, and re-layouts  49.7 us (12%)
  matrix products  48 us (11%)
  other arithmetic  22.5 us (5%)
  starting transfers between devices  7.87 us (2%)
    ppermute x1, waiting for transfers between devices, from_partner(): lax.ppermute(value, axis, [(i, i ^ 1 << stride) for i in range(lax.axis_s...  180 us
    all_to_all x1, blocking collectives, per_device(): lax.all_to_all(spectra, 'tm', split_axis=0, concat_axis=2, tiled=True)  108 us
    dot_general x1, matrix products, per_device(): jnp.einsum('isn,crn->crsi', filtered, table, preferred_element_type=jnp.f...  16.6 us
    dot_general x1, matrix products, cross_power(): jnp.einsum('crsi,crsj->cij', rows, cols, preferred_element_type=jnp.float32)  15.7 us
    dot_general x1, matrix products, cross_power(): jnp.einsum('crsi,crsj->cij', rows, rotated, preferred_element_type=jnp.fl...  15.7 us
    ppermute x1, waiting for transfers between devices, from_behind(): return lax.ppermute(value, axis, pairs)  15.1 us
    convert_element_type x1, local copies, waits for them, and re-layouts, per_device(): spectra = jnp.einsum('isn,crn->crsi', filtered, table, preferred_element_...  11.5 us
  transfers between devices with their start and end apart: 2, of which 2 were waited for; matrix products, arithmetic and copies ran while one was open for 1% of the time, Pallas kernels for 0%

commit v1 on v0

v1 whole, which is shorter than its diff:
```python
import functools
import math

import jax
import jax.numpy as jnp
from jax import lax
from jax.experimental import pallas as pl
from jax.experimental.pallas import tpu as pltpu
from jax.sharding import PartitionSpec as P

MESH = pl.DeviceIdType.MESH
F32 = jnp.float32
BF16 = jnp.bfloat16
CHUNK = 128
CHUNKS = 4
PARTS = 2 * CHUNKS
FRAMES = 16
NFFT = 512
TAPS = 4
GROUP = 512


def table_rows(length):
    row = jnp.arange(length, dtype=jnp.int32)[:, None]
    n = jnp.arange(length, dtype=jnp.int32)[None, :]
    place, k, z, r = row // 16, row // 8 % 2, row // 2 % 4, row % 2
    channel = 4 * (z % 2 * 32 + place) + 2 * (z // 2) + k
    phase = (channel * n % length).astype(F32) * (2.0 * math.pi / length)
    norm = 1.0 / math.sqrt(length)
    return jnp.where(r == 0, jnp.cos(phase) * norm, -jnp.sin(phase) * norm).astype(BF16)


def position():
    g, t = lax.axis_index("inp"), lax.axis_index("tm")
    return g, t, g * 2 + t // 32, t // 8 % 4, t // 2 % 4, t % 2


def device(z, x, y, c):
    return (z // 2, z % 2 * 32 + x * 8 + y * 2 + c)


def wait_for(ref, sem):
    pltpu.make_async_copy(ref, ref, sem).wait()


def turn_kernel(
    raw, taps, table, own, got_cross, got_auto,
    ext, filt, freq, at_start, after_x, after_y, turned, cross, auto, stage,
    raw_sem, tail_send, tail_recv, send_sems, recv_sems, res_send, res_recv, out_sem,
):
    g, t, z, x, y, c = position()
    after = (lax.rem(t + 1, 64), lax.rem(t + 63, 64))
    reads = []
    for i in range(CHUNKS):
        rows = pl.ds(i * CHUNK, CHUNK)
        reads.append(
            pltpu.make_async_copy(
                raw.at[rows], ext.at[rows, pl.ds(3 * NFFT, FRAMES * NFFT)], raw_sem.at[i]
            )
        )
        reads[-1].start()

    barrier = pltpu.get_barrier_semaphore()
    along_x = [(z, lax.rem(x + d, 4), y, c) for d in (1, 3, 2)]
    along_y = [(z, x, lax.rem(y + d, 4), c) for d in (1, 3, 2)]
    along_z = [
        (lax.rem(z + d, 4), x, y, lax.rem(c + e, 2))
        for d, e in ((1, 0), (3, 0), (2, 0), (1, 1), (3, 1), (2, 1), (0, 1))
    ]
    for there in along_x + along_y + along_z:
        pl.semaphore_signal(barrier, inc=1, device_id=device(*there), device_id_type=MESH)
    for other in after:
        pl.semaphore_signal(barrier, inc=1, device_id=(g, other), device_id_type=MESH)
    pl.semaphore_wait(barrier, 15)

    tails = []
    for i in range(CHUNKS):
        rows = pl.ds(i * CHUNK, CHUNK)
        tails.append(
            pltpu.make_async_remote_copy(
                src_ref=raw.at[rows, pl.ds((FRAMES - 3) * NFFT, 3 * NFFT)],
                dst_ref=ext.at[rows, pl.ds(0, 3 * NFFT)],
                send_sem=tail_send.at[i],
                recv_sem=tail_recv.at[i],
                device_id=(g, after[0]),
                device_id_type=MESH,
            )
        )
        tails[-1].start()

    to = lax.broadcasted_iota(jnp.int32, (256, 256), 0)
    fro = lax.broadcasted_iota(jnp.int32, (256, 256), 1)
    swap = jnp.where((to // 16 == fro % 16) & (to % 16 == fro // 16), 1.0, 0.0).astype(BF16)

    def transform(i):
        rows = i * CHUNK

        def pair(j, _):
            for half in range(2):
                for b in range(0, CHUNK, 16):
                    total = None
                    for tap in range(TAPS):
                        at = pl.multiple_of((2 * j + half + tap) * NFFT, NFFT)
                        frame = ext[pl.ds(rows + b, 16), pl.ds(at, NFFT)].astype(F32)
                        term = taps[pl.ds(tap, 1), :] * frame
                        total = term if total is None else total + term
                    filt[pl.ds(half * CHUNK + b, 16), :] = total.astype(BF16)
            for m in range(0, NFFT, 256):
                out = lax.dot_general(
                    table[pl.ds(m, 256), :], filt[...], (((1,), (1,)), ((), ())),
                    preferred_element_type=F32,
                ).astype(BF16)
                for half in range(2):
                    freq[2 * j + half, pl.ds(m // 16, 16)] = out[
                        :, half * CHUNK : (half + 1) * CHUNK
                    ].reshape(16, 16, CHUNK)
            return 0

        reads[i].wait()
        lax.fori_loop(2, FRAMES // 2, pair, 0)
        tails[i].wait_recv()

        @pl.when(t == 0)
        def _():
            ext[pl.ds(rows, CHUNK), pl.ds(0, 3 * NFFT)] = jnp.zeros((CHUNK, 3 * NFFT), BF16)

        lax.fori_loop(0, 2, pair, 0)

        def place(d, _):
            px, py = d // 4, d % 4
            both = [freq[:, 2 * d + e].reshape(256, CHUNK) for e in range(2)]
            out = jnp.dot(swap, jnp.concatenate(both, axis=1), preferred_element_type=F32)
            out = out.astype(BF16)
            for e in range(2):
                block = out[:, e * CHUNK : (e + 1) * CHUNK].reshape(2, 4, 2, 16, CHUNK)
                for k in range(2):
                    at_start[2 * i + k, px, py, :, e] = block[k]
            return 0

        lax.fori_loop(0, 16, place, 0)

    def send(step, n, src, dst, there):
        pltpu.make_async_remote_copy(
            src_ref=src, dst_ref=dst, send_sem=send_sems.at[step, n],
            recv_sem=recv_sems.at[step, n], device_id=device(*there), device_id_type=MESH,
        ).start()

    def keep(step, n, src, dst):
        pltpu.make_async_copy(src, dst, recv_sems.at[step, n]).start()

    def step_x(n):
        for there in along_x:
            send(0, n, at_start.at[n, there[1]], after_x.at[n, x], there)
        keep(0, n, at_start.at[n, x], after_x.at[n, x])

    def step_y(n):
        wait_for(after_x.at[n], recv_sems.at[0, n])
        for there in along_y:
            send(1, n, after_x.at[n, :, there[2]], after_y.at[n, :, y], there)
        keep(1, n, after_x.at[n, :, y], after_y.at[n, :, y])

    def step_z(n):
        wait_for(after_y.at[n], recv_sems.at[1, n])
        for there in along_z:
            send(2, n, after_y.at[n, :, :, there[0], there[3]], turned.at[n, :, :, z, c], there)
        keep(2, n, after_y.at[n, :, :, z, c], turned.at[n, :, :, z, c])

    def advance(n):
        if 0 <= n < PARTS:
            step_y(n)
        if 0 <= n - 1 < PARTS:
            step_z(n - 1)

    for i in range(CHUNKS):
        transform(i)
        step_x(2 * i)
        step_x(2 * i + 1)
        if i == 2:
            advance(0)
    for n in range(1, PARTS + 1):
        advance(n)
    for n in range(PARTS):
        wait_for(turned.at[n], recv_sems.at[2, n])

    def columns(k, group, r, first, count):
        parts = [
            turned[2 * i + k, :, :, pl.ds(2 * group, 2), :, r].reshape(1024, CHUNK)
            for i in range(first, first + count)
        ]
        return jnp.concatenate(parts, axis=1)

    def product(a, b):
        return lax.dot_general(a, b, (((0,), (0,)), ((), ())), preferred_element_type=F32)

    scale = 1.0 / 1024.0
    partner = device(lax.rem(z + 2, 4), x, y, c)

    def tile(k, left, right, m):
        a0, a1 = (columns(k, left, r, 2 * m, 2) for r in range(2))
        b0, b1 = (columns(k, right, r, 0, 4) for r in range(2))
        real = (product(a0, b0) + product(a1, b1)) * scale
        imag = (product(a0, b1) - product(a1, b0)) * scale
        return real, imag

    def returned(src, dst, n):
        return pltpu.make_async_remote_copy(
            src_ref=src, dst_ref=dst, send_sem=res_send.at[n], recv_sem=res_recv.at[n],
            device_id=partner, device_id_type=MESH,
        )

    results = []
    for k in range(2):
        for m in range(2):
            rows = pl.ds(m * 256, 256)
            real, imag = tile(k, 1 - g, 1 - g, m)
            i = lax.broadcasted_iota(jnp.int32, (256, GROUP), 0) + m * 256
            j = lax.broadcasted_iota(jnp.int32, (256, GROUP), 1)
            auto[k, rows] = jnp.where(i <= j, real, imag).astype(BF16)
            results.append(returned(auto.at[k, rows], got_auto.at[k, rows], 4 * k + 2 * m))
            results[-1].start()
            real, imag = tile(k, 1 - g, g, m)
            cross[k, m, 0] = real.astype(BF16)
            cross[k, m, 1] = imag.astype(BF16)
            results.append(returned(cross.at[k, m], got_cross.at[k, m], 4 * k + 2 * m + 1))
            results[-1].start()

    writes = []
    for k in range(2):
        for m in range(2):
            for side in range(2):
                n = len(writes)
                if n >= 2:
                    writes[n - 2].wait()
                real, imag = tile(k, g, side, m)
                stage[n % 2, 0] = real
                stage[n % 2, 1] = imag
                writes.append(
                    pltpu.make_async_copy(
                        stage.at[n % 2],
                        own.at[k, :, pl.ds(m * 256, 256), pl.ds(side * GROUP, GROUP)],
                        out_sem.at[n % 2],
                    )
                )
                writes[-1].start()
    for w in writes[-2:]:
        w.wait()
    for i in range(CHUNKS):
        tails[i].wait_send()
    for n in range(PARTS):
        wait_for(at_start.at[n, pl.ds(0, 3)], send_sems.at[0, n])
        wait_for(after_x.at[n, pl.ds(0, 3)], send_sems.at[1, n])
        wait_for(after_y.at[n, :, :, pl.ds(0, 3)], send_sems.at[2, n])
        wait_for(after_y.at[n, :, :, 0, 0], send_sems.at[2, n])
    for r in results:
        r.wait()


def join_kernel(group, own, cross, auto, out):
    step = pl.program_id(0)

    @pl.when(step >= 2)
    def _():
        out[...] = own[...]

    @pl.when(step < 2)
    def _():
        upper = auto[0].astype(F32)
        lower = upper.T
        i = lax.broadcasted_iota(jnp.int32, upper.shape, 0)
        j = lax.broadcasted_iota(jnp.int32, upper.shape, 1)
        real = jnp.where(i <= j, upper, lower)
        imag = jnp.where(i > j, upper, jnp.where(i < j, -lower, 0.0))
        far = cross[0].astype(F32)
        for side in range(2):

            @pl.when(group[0] == side)
            def _():
                mine = pl.ds(side * GROUP, GROUP)
                others = (1 - side) * GROUP
                out[0, 0, :, mine] = real
                out[0, 1, :, mine] = imag
                for m in range(2):
                    for part in range(2):
                        out[0, part, pl.ds(m * 256, 256), pl.ds(others, GROUP)] = far[m, part]


def per_device(raw, taps):
    any_space = pl.BlockSpec(memory_space=pl.ANY)
    vmem = pl.BlockSpec(memory_space=pltpu.VMEM)
    parts = (PARTS, 4, 4, 4, 2, 2, 16, CHUNK)
    own, got_cross, got_auto = pl.pallas_call(
        turn_kernel,
        out_shape=(
            jax.ShapeDtypeStruct((2, 2, GROUP, 2 * GROUP), F32),
            jax.ShapeDtypeStruct((2, 2, 2, 256, GROUP), BF16),
            jax.ShapeDtypeStruct((2, GROUP, GROUP), BF16),
        ),
        in_specs=[any_space, vmem, vmem],
        out_specs=(any_space,) * 3,
        scratch_shapes=[
            pltpu.VMEM((GROUP, (FRAMES + 3) * NFFT), BF16),
            pltpu.VMEM((2 * CHUNK, NFFT), BF16),
            pltpu.VMEM((FRAMES, 32, 16, CHUNK), BF16),
            pltpu.VMEM(parts, BF16),
            pltpu.VMEM(parts, BF16),
            pltpu.VMEM(parts, BF16),
            pltpu.VMEM(parts, BF16),
            pltpu.VMEM((2, 2, 2, 256, GROUP), BF16),
            pltpu.VMEM((2, GROUP, GROUP), BF16),
            pltpu.VMEM((2, 2, 256, GROUP), F32),
            pltpu.SemaphoreType.DMA((CHUNKS,)),
            pltpu.SemaphoreType.DMA((CHUNKS,)),
            pltpu.SemaphoreType.DMA((CHUNKS,)),
            pltpu.SemaphoreType.DMA((3, PARTS)),
            pltpu.SemaphoreType.DMA((3, PARTS)),
            pltpu.SemaphoreType.DMA((8,)),
            pltpu.SemaphoreType.DMA((8,)),
            pltpu.SemaphoreType.DMA((2,)),
        ],
        compiler_params=pltpu.CompilerParams(
            collective_id=0, has_side_effects=True, vmem_limit_bytes=62 * 1024 * 1024
        ),
    )(raw, taps, table_rows(NFFT))

    group = lax.axis_index("inp").astype(jnp.int32).reshape(1)
    return pl.pallas_call(
        join_kernel,
        out_shape=jax.ShapeDtypeStruct((4, 2, GROUP, 2 * GROUP), F32),
        grid_spec=pltpu.PrefetchScalarGridSpec(
            num_scalar_prefetch=1,
            grid=(4,),
            in_specs=[
                pl.BlockSpec(
                    (1, 2, GROUP, 2 * GROUP), lambda i, s: (jnp.maximum(i - 2, 0), 0, 0, 0)
                ),
                pl.BlockSpec(
                    (1, 2, 2, 256, GROUP), lambda i, s: (jnp.minimum(i, 1), 0, 0, 0, 0)
                ),
                pl.BlockSpec((1, GROUP, GROUP), lambda i, s: (jnp.minimum(i, 1), 0, 0)),
            ],
            out_specs=pl.BlockSpec(
                (1, 2, GROUP, 2 * GROUP), lambda i, s: (lax.rem(i + 2 * (1 - s[0]), 4), 0, 0, 0)
            ),
        ),
        compiler_params=pltpu.CompilerParams(vmem_limit_bytes=48 * 1024 * 1024),
    )(group, own, got_cross, got_auto)


def solution(mesh):
    return jax.shard_map(
        per_device,
        mesh=mesh,
        in_specs=(P("inp", "tm"), P()),
        out_specs=P("tm", None, "inp", None),
        check_vma=False,
    )
```

time: 431 us -> 265 us (0.61)
  the two profiles are of different devices: /device:TPU:1 before, /device:TPU:66 now
where the time goes in v1:
time: 265 us
  Pallas kernels  256 us (97%)
  other arithmetic  5.67 us (2%)
  local copies, waits for them, and re-layouts  2.81 us (1%)
    pallas_call x1, Pallas kernels, per_device(): pl.pallas_call(turn_kernel, out_shape=(jax.ShapeDtypeStruct((2, 2, GROUP,...  245 us
    pallas_call x1, Pallas kernels, per_device(): pl.pallas_call(join_kernel, out_shape=jax.ShapeDtypeStruct((4, 2, GROUP,...  11.3 us
    convert_element_type x1, other arithmetic, table_rows(): jnp.where(r == 0, jnp.cos(phase) * norm, -jnp.sin(phase) * norm)  5.65 us

profile of v1, /device:TPU:66, one launch (start us, length us, event | category | flops | bytes accessed | tf_op | source)
XLA Modules:
  0.0 264.8 jit_solution(5768869374191897429)
XLA Ops:
  0.0 5.7 %select_convert_fusion.table = bf16[512,512]{1,0:T(8,128)(2,1)} fusion(s32[512]{0:T(512)S(1)} %fusion.12, pred[512]{0:T(512)(128)(4,1)S(1)} %fusion.6), kind=kLoop, calls=%fused_computation.6 | loop fusion | flops 4980736 | bytes 526848 | tf_op jit(solution)/shard_map/convert_element_type | solution.py:30
  5.7 244.9 %shard_map.28 = (f32[2,2,512,1024]{3,2,1,0:T(8,128)}, bf16[2,2,2,256,512]{4,3,2,1,0:T(8,128)(2,1)}, bf16[2,512,512]{2,1,0:T(8,128)(2,1)}) custom-call(bf16[512,8192]{1,0:T(8,128)(2,1)} %raw.1, f32[4,512]{1,0:T(4,128)} %taps.1, bf16[512,512]{1,0:T(8,128)(2,1)} %select_convert_fusion.table), custom_call_target="tpu_custom_call" | custom-call | tf_op jit(solution)/shard_map/pallas_call | solution.py:291
  250.6 0.0 copy-start
  250.6 1.6 copy-done
  252.2 0.0 copy-start.1
  252.2 1.2 copy-done.1
  253.4 11.3 %shard_map.29 = f32[4,2,512,1024]{3,2,1,0:T(8,128)} custom-call(s32[1]{0:T(128)} %bitcast.group, f32[2,2,512,1024]{3,2,1,0:T(8,128)} %get-tuple-element.8.own, bf16[2,2,2,256,512]{4,3,2,1,0:T(8,128)(2,1)S(1)} %copy-done, bf16[2,512,512]{2,1,0:T(8,128)(2,1)S(1)} %copy-done.1), custom_call_target="tpu_custom_call" | custom-call | tf_op jit(solution)/shard_map/pallas_call | solution.py:326
  (2 shorter events, 0.0 us)
Async XLA Ops:
  250.6 1.6 copy-start
  252.2 1.2 copy-start.1

commit v2 on v1

--- a/solution.py
+++ b/solution.py
@@ -3,6 +3,7 @@
 
 import jax
 import jax.numpy as jnp
+import numpy as np
 from jax import lax
 from jax.experimental import pallas as pl
 from jax.experimental.pallas import tpu as pltpu
@@ -13,21 +14,30 @@
 BF16 = jnp.bfloat16
 CHUNK = 128
 CHUNKS = 4
-PARTS = 2 * CHUNKS
+PARTS = 4 * CHUNKS
 FRAMES = 16
 NFFT = 512
 TAPS = 4
 GROUP = 512
+ORDERS = (
+    "yzx", "xyz", "yxz", "zyx", "zxy", "xzy", "xyz", "xyz",
+    "zyx", "yzx", "xyz", "xzy", "xyz", "zyx", "yxz", "zyx",
+)
+ARRIVALS = (
+    (),
+    ((0, 0), (1, 0), (3, 0),),
+    ((2, 0), (4, 0), (5, 0),),
+    ((1, 1), (0, 1), (6, 0), (3, 1), (7, 0), (8, 0), (9, 0), (5, 1), (10, 0), (14, 0), (11, 0), (13, 0), (6, 1), (2, 1), (15, 0), (7, 1), (4, 1), (8, 1), (9, 1), (12, 0), (11, 1), (10, 1), (13, 1), (14, 1), (15, 1), (12, 1),),
+)
 
 
 def table_rows(length):
-    row = jnp.arange(length, dtype=jnp.int32)[:, None]
-    n = jnp.arange(length, dtype=jnp.int32)[None, :]
-    place, k, z, r = row // 16, row // 8 % 2, row // 2 % 4, row % 2
+    row = np.arange(length)[:, None]
+    place, k, r, z = row // 16, row // 8 % 2, row // 4 % 2, row % 4
     channel = 4 * (z % 2 * 32 + place) + 2 * (z // 2) + k
-    phase = (channel * n % length).astype(F32) * (2.0 * math.pi / length)
-    norm = 1.0 / math.sqrt(length)
-    return jnp.where(r == 0, jnp.cos(phase) * norm, -jnp.sin(phase) * norm).astype(BF16)
+    phase = (channel * np.arange(length)[None, :] % length) * (2.0 * math.pi / length)
+    values = np.where(r == 0, np.cos(phase), -np.sin(phase)) / math.sqrt(length)
+    return jnp.asarray(values.astype(np.float32).astype(BF16))
 
 
 def position():
@@ -45,8 +55,8 @@
 
 def turn_kernel(
     raw, taps, table, own, got_cross, got_auto,
-    ext, filt, freq, at_start, after_x, after_y, turned, cross, auto, stage,
-    raw_sem, tail_send, tail_recv, send_sems, recv_sems, res_send, res_recv, out_sem,
+    ext, filt, freq, at_start, after_one, after_two, turned, cross, auto, stage,
+    raw_sem, tail_send, tail_recv, send_sems, recv_sems, res_send, res_recv, out_sem, ready,
 ):
     g, t, z, x, y, c = position()
     after = (lax.rem(t + 1, 64), lax.rem(t + 63, 64))
@@ -132,9 +142,9 @@
             out = jnp.dot(swap, jnp.concatenate(both, axis=1), preferred_element_type=F32)
             out = out.astype(BF16)
             for e in range(2):
-                block = out[:, e * CHUNK : (e + 1) * CHUNK].reshape(2, 4, 2, 16, CHUNK)
-                for k in range(2):
-                    at_start[2 * i + k, px, py, :, e] = block[k]
+                block = out[:, e * CHUNK : (e + 1) * CHUNK].reshape(4, 4, 16, CHUNK)
+                for q in range(4):
+                    at_start[4 * i + q, px, py, :, e] = block[q]
             return 0
 
         lax.fori_loop(0, 16, place, 0)
@@ -148,43 +158,40 @@
     def keep(step, n, src, dst):
         pltpu.make_async_copy(src, dst, recv_sems.at[step, n]).start()
 
-    def step_x(n):
-        for there in along_x:
-            send(0, n, at_start.at[n, there[1]], after_x.at[n, x], there)
-        keep(0, n, at_start.at[n, x], after_x.at[n, x])
-
-    def step_y(n):
-        wait_for(after_x.at[n], recv_sems.at[0, n])
-        for there in along_y:
-            send(1, n, after_x.at[n, :, there[2]], after_y.at[n, :, y], there)
-        keep(1, n, after_x.at[n, :, y], after_y.at[n, :, y])
-
-    def step_z(n):
-        wait_for(after_y.at[n], recv_sems.at[1, n])
-        for there in along_z:
-            send(2, n, after_y.at[n, :, :, there[0], there[3]], turned.at[n, :, :, z, c], there)
-        keep(2, n, after_y.at[n, :, :, z, c], turned.at[n, :, :, z, c])
-
-    def advance(n):
-        if 0 <= n < PARTS:
-            step_y(n)
-        if 0 <= n - 1 < PARTS:
-            step_z(n - 1)
+    held = (at_start, after_one, after_two, turned)
+    peers = {"x": along_x, "y": along_y, "z": along_z}
+
+    def block(ref, n, dim, there):
+        if dim == "x":
+            return ref.at[n, there[1]]
+        if dim == "y":
+            return ref.at[n, :, there[2]]
+        return ref.at[n, :, :, there[0], there[3]]
+
+    def exchange(n, step):
+        dim = ORDERS[n][step]
+        mine = block(held[step + 1], n, dim, (z, x, y, c))
+        for there in peers[dim]:
+            send(step, n, block(held[step], n, dim, there), mine, there)
+        keep(step, n, block(held[step], n, dim, (z, x, y, c)), mine)
 
     for i in range(CHUNKS):
         transform(i)
-        step_x(2 * i)
-        step_x(2 * i + 1)
-        if i == 2:
-            advance(0)
-    for n in range(1, PARTS + 1):
-        advance(n)
+        for n in range(4 * i, 4 * i + 4):
+            exchange(n, 0)
+        for n, step in ARRIVALS[i]:
+            wait_for(held[step + 1].at[n], recv_sems.at[step, n])
+            exchange(n, step + 1)
     for n in range(PARTS):
         wait_for(turned.at[n], recv_sems.at[2, n])
 
+    for there in along_z:
+        pl.semaphore_signal(ready, inc=1, device_id=device(*there), device_id_type=MESH)
+    pl.semaphore_wait(ready, 7)
+
     def columns(k, group, r, first, count):
         parts = [
-            turned[2 * i + k, :, :, pl.ds(2 * group, 2), :, r].reshape(1024, CHUNK)
+            turned[4 * i + 2 * k + r, :, :, pl.ds(2 * group, 2)].reshape(1024, CHUNK)
             for i in range(first, first + count)
         ]
         return jnp.concatenate(parts, axis=1)
@@ -247,10 +254,15 @@
     for i in range(CHUNKS):
         tails[i].wait_send()
     for n in range(PARTS):
-        wait_for(at_start.at[n, pl.ds(0, 3)], send_sems.at[0, n])
-        wait_for(after_x.at[n, pl.ds(0, 3)], send_sems.at[1, n])
-        wait_for(after_y.at[n, :, :, pl.ds(0, 3)], send_sems.at[2, n])
-        wait_for(after_y.at[n, :, :, 0, 0], send_sems.at[2, n])
+        for step in range(3):
+            sent = held[step].at[n]
+            if ORDERS[n][step] == "x":
+                wait_for(sent.at[pl.ds(0, 3)], send_sems.at[step, n])
+            elif ORDERS[n][step] == "y":
+                wait_for(sent.at[:, pl.ds(0, 3)], send_sems.at[step, n])
+            else:
+                wait_for(sent.at[:, :, pl.ds(0, 3)], send_sems.at[step, n])
+                wait_for(sent.at[:, :, 0, 0], send_sems.at[step, n])
     for r in results:
         r.wait()
 
@@ -287,7 +299,7 @@
 def per_device(raw, taps):
     any_space = pl.BlockSpec(memory_space=pl.ANY)
     vmem = pl.BlockSpec(memory_space=pltpu.VMEM)
-    parts = (PARTS, 4, 4, 4, 2, 2, 16, CHUNK)
+    parts = (PARTS, 4, 4, 4, 2, 16, CHUNK)
     own, got_cross, got_auto = pl.pallas_call(
         turn_kernel,
         out_shape=(
@@ -316,6 +328,7 @@
             pltpu.SemaphoreType.DMA((8,)),
             pltpu.SemaphoreType.DMA((8,)),
             pltpu.SemaphoreType.DMA((2,)),
+            pltpu.SemaphoreType.REGULAR,
         ],
         compiler_params=pltpu.CompilerParams(
             collective_id=0, has_side_effects=True, vmem_limit_bytes=62 * 1024 * 1024

time: 265 us -> 210 us (0.79)
  the two profiles are of different devices: /device:TPU:66 before, /device:TPU:1 now
where the time goes in v2:
time: 210 us; the launch traced here: 209 us
  Pallas kernels  207 us (99%)
  local copies, waits for them, and re-layouts  2.81 us (1%)
    pallas_call x1, Pallas kernels, per_device(): pl.pallas_call(turn_kernel, out_shape=(jax.ShapeDtypeStruct((2, 2, GROUP,...  195 us
    pallas_call x1, Pallas kernels, per_device(): pl.pallas_call(join_kernel, out_shape=jax.ShapeDtypeStruct((4, 2, GROUP,...  11.3 us

profile of v2, /device:TPU:1, one launch (start us, length us, event | category | flops | bytes accessed | tf_op | source)
XLA Modules:
  0.0 209.5 jit_solution(16466651441891643097)
XLA Ops:
  0.0 195.3 %shard_map.37 = (f32[2,2,512,1024]{3,2,1,0:T(8,128)}, bf16[2,2,2,256,512]{4,3,2,1,0:T(8,128)(2,1)}, bf16[2,512,512]{2,1,0:T(8,128)(2,1)}) custom-call(bf16[512,8192]{1,0:T(8,128)(2,1)} %raw.1, f32[4,512]{1,0:T(4,128)} %taps.1, bf16[512,512]{1,0:T(8,128)(2,1)} %constant.8.clone.table), custom_call_target="tpu_custom_call" | custom-call | tf_op jit(solution)/shard_map/pallas_call | solution.py:303
  195.3 0.0 copy-start
  195.3 1.6 copy-done
  196.9 0.0 copy-start.1
  196.9 1.2 copy-done.1
  198.1 11.3 %shard_map.38 = f32[4,2,512,1024]{3,2,1,0:T(8,128)} custom-call(s32[1]{0:T(128)} %bitcast.group, f32[2,2,512,1024]{3,2,1,0:T(8,128)} %get-tuple-element.8.own, bf16[2,2,2,256,512]{4,3,2,1,0:T(8,128)(2,1)S(1)} %copy-done, bf16[2,512,512]{2,1,0:T(8,128)(2,1)S(1)} %copy-done.1), custom_call_target="tpu_custom_call" | custom-call | tf_op jit(solution)/shard_map/pallas_call | solution.py:339
Async XLA Ops:
  195.3 1.6 copy-start
  196.9 1.2 copy-start.1

commit v3 on v2

--- a/solution.py
+++ b/solution.py
@@ -267,33 +267,54 @@
         r.wait()
 
 
-def join_kernel(group, own, cross, auto, out):
-    step = pl.program_id(0)
-
-    @pl.when(step >= 2)
-    def _():
-        out[...] = own[...]
-
-    @pl.when(step < 2)
-    def _():
-        upper = auto[0].astype(F32)
-        lower = upper.T
-        i = lax.broadcasted_iota(jnp.int32, upper.shape, 0)
-        j = lax.broadcasted_iota(jnp.int32, upper.shape, 1)
-        real = jnp.where(i <= j, upper, lower)
-        imag = jnp.where(i > j, upper, jnp.where(i < j, -lower, 0.0))
-        far = cross[0].astype(F32)
-        for side in range(2):
-
-            @pl.when(group[0] == side)
-            def _():
-                mine = pl.ds(side * GROUP, GROUP)
-                others = (1 - side) * GROUP
-                out[0, 0, :, mine] = real
-                out[0, 1, :, mine] = imag
-                for m in range(2):
-                    for part in range(2):
-                        out[0, part, pl.ds(m * 256, 256), pl.ds(others, GROUP)] = far[m, part]
+def join_kernel(own, cross, auto, out, near, far, packed, mine, others, in_sem, own_sem, out_sem):
+    g = lax.axis_index("inp")
+    reads = []
+    for k in range(2):
+        reads.append(pltpu.make_async_copy(auto.at[k], packed.at[k], in_sem.at[k, 0]))
+        reads.append(pltpu.make_async_copy(cross.at[k], far.at[k], in_sem.at[k, 1]))
+    moves, writes = [], []
+    for n in range(4):
+        rows = pl.ds(n % 2 * 256, 256)
+        moves.append(
+            (
+                pltpu.make_async_copy(own.at[n // 2, :, rows], near.at[n], own_sem.at[n]),
+                pltpu.make_async_copy(near.at[n], out.at[2 * g + n // 2, :, rows], out_sem.at[0, n]),
+            )
+        )
+    for copy in reads:
+        copy.start()
+    for read, _ in moves:
+        read.start()
+    for n in range(4):
+        k, m = n // 2, n % 2
+        if m == 0:
+            reads[2 * k].wait()
+            reads[2 * k + 1].wait()
+        rows = pl.ds(m * 256, 256)
+        here = packed[k, m * 256 : (m + 1) * 256, :].astype(F32)
+        flip = packed[k, :, m * 256 : (m + 1) * 256].astype(F32).T
+        i = lax.broadcasted_iota(jnp.int32, here.shape, 0) + m * 256
+        j = lax.broadcasted_iota(jnp.int32, here.shape, 1)
+        mine[n, 0] = jnp.where(i <= j, here, flip)
+        mine[n, 1] = jnp.where(i > j, here, jnp.where(i < j, -flip, 0.0))
+        others[n] = far[k, m].astype(F32)
+        for side, held in ((g, mine), (1 - g, others)):
+            columns = pl.ds(pl.multiple_of(side * GROUP, GROUP), GROUP)
+            writes.append(
+                pltpu.make_async_copy(
+                    held.at[n],
+                    out.at[2 * (1 - g) + k, :, rows, columns],
+                    out_sem.at[1 + len(writes) % 2, n],
+                )
+            )
+            writes[-1].start()
+        moves[n][0].wait()
+        moves[n][1].start()
+    for copy in writes:
+        copy.wait()
+    for _, write in moves:
+        write.wait()
 
 
 def per_device(raw, taps):
@@ -335,28 +356,23 @@
         ),
     )(raw, taps, table_rows(NFFT))
 
-    group = lax.axis_index("inp").astype(jnp.int32).reshape(1)
     return pl.pallas_call(
         join_kernel,
         out_shape=jax.ShapeDtypeStruct((4, 2, GROUP, 2 * GROUP), F32),
-        grid_spec=pltpu.PrefetchScalarGridSpec(
-            num_scalar_prefetch=1,
-            grid=(4,),
-            in_specs=[
-                pl.BlockSpec(
-                    (1, 2, GROUP, 2 * GROUP), lambda i, s: (jnp.maximum(i - 2, 0), 0, 0, 0)
-                ),
-                pl.BlockSpec(
-                    (1, 2, 2, 256, GROUP), lambda i, s: (jnp.minimum(i, 1), 0, 0, 0, 0)
-                ),
-                pl.BlockSpec((1, GROUP, GROUP), lambda i, s: (jnp.minimum(i, 1), 0, 0)),
-            ],
-            out_specs=pl.BlockSpec(
-                (1, 2, GROUP, 2 * GROUP), lambda i, s: (lax.rem(i + 2 * (1 - s[0]), 4), 0, 0, 0)
-            ),
-        ),
-        compiler_params=pltpu.CompilerParams(vmem_limit_bytes=48 * 1024 * 1024),
-    )(group, own, got_cross, got_auto)
+        in_specs=[any_space] * 3,
+        out_specs=any_space,
+        scratch_shapes=[
+            pltpu.VMEM((4, 2, 256, 2 * GROUP), F32),
+            pltpu.VMEM((2, 2, 2, 256, GROUP), BF16),
+            pltpu.VMEM((2, GROUP, GROUP), BF16),
+            pltpu.VMEM((4, 2, 256, GROUP), F32),
+            pltpu.VMEM((4, 2, 256, GROUP), F32),
+            pltpu.SemaphoreType.DMA((2, 2)),
+            pltpu.SemaphoreType.DMA((4,)),
+            pltpu.SemaphoreType.DMA((3, 4)),
+        ],
+        compiler_params=pltpu.CompilerParams(vmem_limit_bytes=62 * 1024 * 1024),
+    )(own, got_cross, got_auto)
 
 
 def solution(mesh):

time: 210 us -> 205 us (0.976)
  Pallas kernels: 207 us -> 204 us
  local copies, waits for them, and re-layouts: 2.81 us -> 0 us
    unnamed x4 -> x0, local copies, waits for them, and re-layouts: 2.81 us -> none
    pallas_call x1, Pallas kernels: 11.3 us -> 8.94 us  [per_device(): pl.pallas_call(join_kernel, out_shape=jax.ShapeDtypeStruct((4, 2, GROUP,...]
where the time goes in v3:
time: 205 us; the launch traced here: 204 us
  Pallas kernels  204 us (100%)
    pallas_call x1, Pallas kernels, per_device(): pl.pallas_call(turn_kernel, out_shape=(jax.ShapeDtypeStruct((2, 2, GROUP,...  195 us
    pallas_call x1, Pallas kernels, per_device(): pl.pallas_call(join_kernel, out_shape=jax.ShapeDtypeStruct((4, 2, GROUP,...  8.94 us

profile of v3, /device:TPU:1, one launch (start us, length us, event | category | flops | bytes accessed | tf_op | source)
XLA Modules:
  0.0 204.4 jit_solution(2449323663979676356)
XLA Ops:
  0.0 195.3 %shard_map.37 = (f32[2,2,512,1024]{3,2,1,0:T(8,128)}, bf16[2,2,2,256,512]{4,3,2,1,0:T(8,128)(2,1)}, bf16[2,512,512]{2,1,0:T(8,128)(2,1)}) custom-call(bf16[512,8192]{1,0:T(8,128)(2,1)} %raw.1, f32[4,512]{1,0:T(4,128)} %taps.1, bf16[512,512]{1,0:T(8,128)(2,1)} %constant.2.clone.table), custom_call_target="tpu_custom_call" | custom-call | tf_op jit(solution)/shard_map/pallas_call | solution.py:324
  195.3 8.9 %shard_map.38 = f32[4,2,512,1024]{3,2,1,0:T(8,128)} custom-call(f32[2,2,512,1024]{3,2,1,0:T(8,128)} %get-tuple-element.8.own, bf16[2,2,2,256,512]{4,3,2,1,0:T(8,128)(2,1)} %get-tuple-element.9.cross, bf16[2,512,512]{2,1,0:T(8,128)(2,1)} %get-tuple-element.10.auto), custom_call_target="tpu_custom_call" | custom-call | tf_op jit(solution)/shard_map/pallas_call | solution.py:359

commit v4 on v3

--- a/solution.py
+++ b/solution.py
@@ -20,14 +20,19 @@
 TAPS = 4
 GROUP = 512
 ORDERS = (
-    "yzx", "xyz", "yxz", "zyx", "zxy", "xzy", "xyz", "xyz",
-    "zyx", "yzx", "xyz", "xzy", "xyz", "zyx", "yxz", "zyx",
+    "xzy", "yzx", "zyx", "zyx", "xyz", "zyx", "yzx", "xyz",
+    "xzy", "zxy", "xzy", "zxy", "xyz", "xyz", "xyz", "zyx",
 )
-ARRIVALS = (
-    (),
-    ((0, 0), (1, 0), (3, 0),),
-    ((2, 0), (4, 0), (5, 0),),
-    ((1, 1), (0, 1), (6, 0), (3, 1), (7, 0), (8, 0), (9, 0), (5, 1), (10, 0), (14, 0), (11, 0), (13, 0), (6, 1), (2, 1), (15, 0), (7, 1), (4, 1), (8, 1), (9, 1), (12, 0), (11, 1), (10, 1), (13, 1), (14, 1), (15, 1), (12, 1),),
+PLAN = (
+    ("F", 0), ("S", 0), ("S", 2), ("S", 1), ("S", 3), ("F", 1), ("S", 4), ("S", 5), ("S", 6),
+    ("F", 2), ("S", 9), ("S", 8), ("S", 10), ("S", 11), ("S", 7), ("W", 0, 0), ("W", 1, 0),
+    ("W", 2, 0), ("W", 3, 0), ("F", 3), ("S", 13), ("S", 12), ("S", 15), ("S", 14), ("W", 4, 0),
+    ("W", 6, 0), ("W", 5, 0), ("W", 2, 1), ("W", 8, 0), ("W", 9, 0), ("W", 3, 1), ("W", 10, 0),
+    ("W", 11, 0), ("W", 4, 1), ("W", 7, 0), ("W", 0, 1), ("W", 5, 1), ("W", 13, 0), ("W", 1, 1),
+    ("W", 7, 1), ("W", 12, 0), ("W", 15, 0), ("W", 14, 0), ("W", 6, 1), ("W", 13, 1), ("W", 8, 1),
+    ("W", 9, 1), ("W", 12, 1), ("W", 10, 1), ("W", 15, 1), ("W", 11, 1), ("W", 14, 1), ("K", 0),
+    ("T", 0, 0), ("T", 0, 1), ("T", 0, 2), ("T", 0, 3), ("K", 1), ("T", 1, 0), ("T", 1, 1),
+    ("T", 1, 2), ("T", 1, 3),
 )
 
 
@@ -175,20 +180,6 @@
             send(step, n, block(held[step], n, dim, there), mine, there)
         keep(step, n, block(held[step], n, dim, (z, x, y, c)), mine)
 
-    for i in range(CHUNKS):
-        transform(i)
-        for n in range(4 * i, 4 * i + 4):
-            exchange(n, 0)
-        for n, step in ARRIVALS[i]:
-            wait_for(held[step + 1].at[n], recv_sems.at[step, n])
-            exchange(n, step + 1)
-    for n in range(PARTS):
-        wait_for(turned.at[n], recv_sems.at[2, n])
-
-    for there in along_z:
-        pl.semaphore_signal(ready, inc=1, device_id=device(*there), device_id_type=MESH)
-    pl.semaphore_wait(ready, 7)
-
     def columns(k, group, r, first, count):
         parts = [
             turned[4 * i + 2 * k + r, :, :, pl.ds(2 * group, 2)].reshape(1024, CHUNK)
@@ -215,21 +206,47 @@
             device_id=partner, device_id_type=MESH,
         )
 
+    def gather(k):
+        for n in range(PARTS):
+            if n // 2 % 2 == k:
+                wait_for(turned.at[n], recv_sems.at[2, n])
+        for there in along_z:
+            pl.semaphore_signal(
+                ready.at[k], inc=1, device_id=device(*there), device_id_type=MESH
+            )
+        pl.semaphore_wait(ready.at[k], 7)
+
     results = []
-    for k in range(2):
-        for m in range(2):
-            rows = pl.ds(m * 256, 256)
+
+    def give(k, block):
+        m = block // 2
+        rows = pl.ds(m * 256, 256)
+        if block % 2 == 0:
             real, imag = tile(k, 1 - g, 1 - g, m)
             i = lax.broadcasted_iota(jnp.int32, (256, GROUP), 0) + m * 256
             j = lax.broadcasted_iota(jnp.int32, (256, GROUP), 1)
             auto[k, rows] = jnp.where(i <= j, real, imag).astype(BF16)
-            results.append(returned(auto.at[k, rows], got_auto.at[k, rows], 4 * k + 2 * m))
-            results[-1].start()
+            results.append(returned(auto.at[k, rows], got_auto.at[k, rows], 4 * k + block))
+        else:
             real, imag = tile(k, 1 - g, g, m)
             cross[k, m, 0] = real.astype(BF16)
             cross[k, m, 1] = imag.astype(BF16)
-            results.append(returned(cross.at[k, m], got_cross.at[k, m], 4 * k + 2 * m + 1))
-            results[-1].start()
+            results.append(returned(cross.at[k, m], got_cross.at[k, m], 4 * k + block))
+        results[-1].start()
+
+    for kind, *at in PLAN:
+        if kind == "F":
+            transform(*at)
+        elif kind == "S":
+            exchange(at[0], 0)
+        elif kind == "W":
+            n, step = at
+            wait_for(held[step + 1].at[n], recv_sems.at[step, n])
+            exchange(n, step + 1)
+        elif kind == "K":
+            gather(*at)
+        else:
+            give(*at)
 
     writes = []
     for k in range(2):
@@ -349,7 +366,7 @@
             pltpu.SemaphoreType.DMA((8,)),
             pltpu.SemaphoreType.DMA((8,)),
             pltpu.SemaphoreType.DMA((2,)),
-            pltpu.SemaphoreType.REGULAR,
+            pltpu.SemaphoreType.REGULAR((2,)),
         ],
         compiler_params=pltpu.CompilerParams(
             collective_id=0, has_side_effects=True, vmem_limit_bytes=62 * 1024 * 1024

time: 205 us -> 198 us (0.966)
  Pallas kernels: 204 us -> 197 us
    pallas_call x1, Pallas kernels: 195 us -> 188 us  [per_device(): pl.pallas_call(turn_kernel, out_shape=(jax.ShapeDtypeStruct((2, 2, GROUP,...]
where the time goes in v4:
time: 198 us
  Pallas kernels  197 us (99%)
    pallas_call x1, Pallas kernels, per_device(): pl.pallas_call(turn_kernel, out_shape=(jax.ShapeDtypeStruct((2, 2, GROUP,...  188 us
    pallas_call x1, Pallas kernels, per_device(): pl.pallas_call(join_kernel, out_shape=jax.ShapeDtypeStruct((4, 2, GROUP,...  8.94 us

profile of v4, /device:TPU:1, one launch (start us, length us, event | category | flops | bytes accessed | tf_op | source)
XLA Modules:
  0.0 197.6 jit_solution(12973360406356926170)
XLA Ops:
  0.0 188.5 %shard_map.37 = (f32[2,2,512,1024]{3,2,1,0:T(8,128)}, bf16[2,2,2,256,512]{4,3,2,1,0:T(8,128)(2,1)}, bf16[2,512,512]{2,1,0:T(8,128)(2,1)}) custom-call(bf16[512,8192]{1,0:T(8,128)(2,1)} %raw.1, f32[4,512]{1,0:T(4,128)} %taps.1, bf16[512,512]{1,0:T(8,128)(2,1)} %constant.2.clone.table), custom_call_target="tpu_custom_call" | custom-call | tf_op jit(solution)/shard_map/pallas_call | solution.py:341
  188.5 8.9 %shard_map.38 = f32[4,2,512,1024]{3,2,1,0:T(8,128)} custom-call(f32[2,2,512,1024]{3,2,1,0:T(8,128)} %get-tuple-element.8.own, bf16[2,2,2,256,512]{4,3,2,1,0:T(8,128)(2,1)} %get-tuple-element.9.cross, bf16[2,512,512]{2,1,0:T(8,128)(2,1)} %get-tuple-element.10.auto), custom_call_target="tpu_custom_call" | custom-call | tf_op jit(solution)/shard_map/pallas_call | solution.py:376

commit v5 on v4

--- a/solution.py
+++ b/solution.py
@@ -59,9 +59,9 @@
 
 
 def turn_kernel(
-    raw, taps, table, own, got_cross, got_auto,
-    ext, filt, freq, at_start, after_one, after_two, turned, cross, auto, stage,
-    raw_sem, tail_send, tail_recv, send_sems, recv_sems, res_send, res_recv, out_sem, ready,
+    raw, taps, rows_hbm, own, got_cross, got_auto,
+    ext, table, filt, freq, at_start, after_one, after_two, turned, cross, auto, stage,
+    raw_sem, table_sem, tail_send, tail_recv, send_sems, recv_sems, res_send, res_recv, out_sem, ready,
 ):
     g, t, z, x, y, c = position()
     after = (lax.rem(t + 1, 64), lax.rem(t + 63, 64))
@@ -74,6 +74,9 @@
             )
         )
         reads[-1].start()
+
+    fetch = pltpu.make_async_copy(rows_hbm, table, table_sem)
+    fetch.start()
 
     barrier = pltpu.get_barrier_semaphore()
     along_x = [(z, lax.rem(x + d, 4), y, c) for d in (1, 3, 2)]
@@ -234,6 +237,7 @@
             results.append(returned(cross.at[k, m], got_cross.at[k, m], 4 * k + block))
         results[-1].start()
 
+    fetch.wait()
     for kind, *at in PLAN:
         if kind == "F":
             transform(*at)
@@ -256,8 +260,8 @@
                 if n >= 2:
                     writes[n - 2].wait()
                 real, imag = tile(k, g, side, m)
-                stage[n % 2, 0] = real
-                stage[n % 2, 1] = imag
+                stage[n % 2, 0] = real.astype(BF16)
+                stage[n % 2, 1] = imag.astype(BF16)
                 writes.append(
                     pltpu.make_async_copy(
                         stage.at[n % 2],
@@ -284,7 +288,7 @@
         r.wait()
 
 
-def join_kernel(own, cross, auto, out, near, far, packed, mine, others, in_sem, own_sem, out_sem):
+def join_kernel(own, cross, auto, out, near, wide, far, packed, mine, others, in_sem, own_sem, out_sem):
     g = lax.axis_index("inp")
     reads = []
     for k in range(2):
@@ -296,7 +300,7 @@
         moves.append(
             (
                 pltpu.make_async_copy(own.at[n // 2, :, rows], near.at[n], own_sem.at[n]),
-                pltpu.make_async_copy(near.at[n], out.at[2 * g + n // 2, :, rows], out_sem.at[0, n]),
+                pltpu.make_async_copy(wide.at[n], out.at[2 * g + n // 2, :, rows], out_sem.at[0, n]),
             )
         )
     for copy in reads:
@@ -327,6 +331,7 @@
             )
             writes[-1].start()
         moves[n][0].wait()
+        wide[n] = near[n].astype(F32)
         moves[n][1].start()
     for copy in writes:
         copy.wait()
@@ -341,14 +346,15 @@
     own, got_cross, got_auto = pl.pallas_call(
         turn_kernel,
         out_shape=(
-            jax.ShapeDtypeStruct((2, 2, GROUP, 2 * GROUP), F32),
+            jax.ShapeDtypeStruct((2, 2, GROUP, 2 * GROUP), BF16),
             jax.ShapeDtypeStruct((2, 2, 2, 256, GROUP), BF16),
             jax.ShapeDtypeStruct((2, GROUP, GROUP), BF16),
         ),
-        in_specs=[any_space, vmem, vmem],
+        in_specs=[any_space, vmem, any_space],
         out_specs=(any_space,) * 3,
         scratch_shapes=[
             pltpu.VMEM((GROUP, (FRAMES + 3) * NFFT), BF16),
+            pltpu.VMEM((NFFT, NFFT), BF16),
             pltpu.VMEM((2 * CHUNK, NFFT), BF16),
             pltpu.VMEM((FRAMES, 32, 16, CHUNK), BF16),
             pltpu.VMEM(parts, BF16),
@@ -357,8 +363,9 @@
             pltpu.VMEM(parts, BF16),
             pltpu.VMEM((2, 2, 2, 256, GROUP), BF16),
             pltpu.VMEM((2, GROUP, GROUP), BF16),
-            pltpu.VMEM((2, 2, 256, GROUP), F32),
+            pltpu.VMEM((2, 2, 256, GROUP), BF16),
             pltpu.SemaphoreType.DMA((CHUNKS,)),
+            pltpu.SemaphoreType.DMA,
             pltpu.SemaphoreType.DMA((CHUNKS,)),
             pltpu.SemaphoreType.DMA((CHUNKS,)),
             pltpu.SemaphoreType.DMA((3, PARTS)),
@@ -379,6 +386,7 @@
         in_specs=[any_space] * 3,
         out_specs=any_space,
         scratch_shapes=[
+            pltpu.VMEM((4, 2, 256, 2 * GROUP), BF16),
             pltpu.VMEM((4, 2, 256, 2 * GROUP), F32),
             pltpu.VMEM((2, 2, 2, 256, GROUP), BF16),
             pltpu.VMEM((2, GROUP, GROUP), BF16),

time: 198 us -> 196 us (0.990)
  no operation moved by 1% of the time
where the time goes in v5:
time: 196 us
  Pallas kernels  196 us (100%)
    pallas_call x1, Pallas kernels, per_device(): pl.pallas_call(turn_kernel, out_shape=(jax.ShapeDtypeStruct((2, 2, GROUP,...  188 us
    pallas_call x1, Pallas kernels, per_device(): pl.pallas_call(join_kernel, out_shape=jax.ShapeDtypeStruct((4, 2, GROUP,...  7.98 us

profile of v5, /device:TPU:1, one launch (start us, length us, event | category | flops | bytes accessed | tf_op | source)
XLA Modules:
  0.0 196.3 jit_solution(1973626410985014821)
XLA Ops:
  0.0 188.1 %shard_map.37 = (bf16[2,2,512,1024]{3,2,1,0:T(8,128)(2,1)}, bf16[2,2,2,256,512]{4,3,2,1,0:T(8,128)(2,1)}, bf16[2,512,512]{2,1,0:T(8,128)(2,1)}) custom-call(bf16[512,8192]{1,0:T(8,128)(2,1)} %raw.1, f32[4,512]{1,0:T(4,128)} %taps.1, bf16[512,512]{1,0:T(8,128)(2,1)} %constant.2.clone.rows_hbm), custom_call_target="tpu_custom_call" | custom-call | tf_op jit(solution)/shard_map/pallas_call | solution.py:346
  188.1 8.0 %shard_map.38 = f32[4,2,512,1024]{3,2,1,0:T(8,128)} custom-call(bf16[2,2,512,1024]{3,2,1,0:T(8,128)(2,1)} %get-tuple-element.8.own, bf16[2,2,2,256,512]{4,3,2,1,0:T(8,128)(2,1)} %get-tuple-element.9.cross, bf16[2,512,512]{2,1,0:T(8,128)(2,1)} %get-tuple-element.10.auto), custom_call_target="tpu_custom_call" | custom-call | tf_op jit(solution)/shard_map/pallas_call | solution.py:383
